TPU v7x, 512 devices: a whole 4x8x8 slice. The times are simulated.
512 devices in a mesh: chan: 128 (over z, x, y_lo), rep: 4 (over y_hi, core).
Axes of the slice: x: 4, y: 8 (y_hi: 2, y_lo: 4; y = y_hi * 4 + y_lo), z: 8, core: 2. Of those that a mesh axis runs over, the one named last changes fastest.
Arguments:
- strain: bfloat16 [2048, 131072], P('chan', 'rep'), may hold values from -60 to 60
- fir_taps: float32 [60], replicated, may hold values from -0.75 to 0.75
- spatial: float32 [9], replicated, may hold values from -2 to 2
Outputs:
- cross_tiles: float32 [2048, 5, 32, 32], P('chan', None, 'rep')
All inputs are finite; a program needn't handle non-finite values.
Results may differ from a plain program's by a relative error of at most 0.0023.
Values may be sent and summed in bfloat16 or wider, within the bound.
A program may use at most 64 MiB of HBM per device.

v0:
```python
import math

import jax
import jax.numpy as jnp
from jax import lax
from jax.sharding import PartitionSpec as P

NFFT = 1024
BINS = 32
FIRST_BIN = 16
STEPS = 4


epsilon = 1e-05


def passed_along(shard, axis, by):
    count = lax.axis_size(axis)
    pairs = [(i, i + by) for i in range(count) if 0 <= i + by < count]
    return lax.ppermute(shard, axis, pairs)


def padded_2(cells, sides, width):
    for axis, dim in sides:
        count = lax.axis_size(axis)
        ends = count - 1
        head = lax.slice_in_dim(cells, 0, width, axis=dim)
        tail = lax.slice_in_dim(cells, cells.shape[dim] - width, cells.shape[dim], axis=dim)
        cells = jnp.concatenate(
            [
                lax.ppermute(tail, axis, [(i, (i + 1) % count) for i in range(ends)]),
                cells,
                lax.ppermute(head, axis, [((i + 1) % count, i) for i in range(ends)]),
            ],
            axis=dim,
        )
    return cells


def from_behind(block, axis, distance):
    devices = range(lax.axis_size(axis))
    route = [((i - distance) % len(devices), i) for i in devices]
    return lax.ppermute(block, axis, route)


def toeplitz_pair(fir_taps):
    source_pos = jnp.arange(128, dtype=jnp.int32)[:, None]
    target_pos = jnp.arange(128, dtype=jnp.int32)[None, :]
    tap_slots = jnp.arange(fir_taps.shape[0], dtype=jnp.int32)
    lag_now = (target_pos - source_pos)[:, :, None]
    lag_before = (target_pos + 128 - source_pos)[:, :, None]
    zero_value = jnp.zeros((), fir_taps.dtype)
    taps_now = jnp.sum(jnp.where(lag_now == tap_slots, fir_taps, zero_value), axis=2)
    taps_before = jnp.sum(jnp.where(lag_before == tap_slots, fir_taps, zero_value), axis=2)
    return (taps_now, taps_before)


def dft_table(bin_count, first_bin, dft_length, float_type):
    sample_pos = jnp.arange(dft_length, dtype=jnp.int32)[:, None]
    freq_bins = (first_bin + jnp.arange(bin_count, dtype=jnp.int32))[None, :]
    phase_index = sample_pos * freq_bins % dft_length
    phase_angle = phase_index.astype(float_type) * (2.0 * math.pi / dft_length)
    inverse_root = 1.0 / math.sqrt(dft_length)
    return jnp.concatenate([jnp.cos(phase_angle), -jnp.sin(phase_angle)], axis=1) * inverse_root


def window_spectra(channel_rows, spatial, taps_now, taps_before, dft_matrix):
    filter_span = spatial.shape[0]
    row_count = channel_rows.shape[0] - filter_span + 1
    mixed_rows = spatial[0] * channel_rows[0:row_count]
    for offset in range(1, filter_span):
        mixed_rows = mixed_rows + spatial[offset] * channel_rows[offset : offset + row_count]
    time_blocks = mixed_rows.reshape(row_count, -1, 128)
    band_pass = jnp.einsum(
        "cbj,ji->cbi", time_blocks[:, 1:], taps_now, precision=lax.Precision.HIGHEST
    )
    band_pass = band_pass + jnp.einsum(
        "cbj,ji->cbi", time_blocks[:, :-1], taps_before, precision=lax.Precision.HIGHEST
    )
    window_data = band_pass.reshape(row_count, -1, dft_matrix.shape[0])
    window_power = jnp.mean(window_data * window_data, axis=2, keepdims=True)
    normalized = window_data / jnp.sqrt(window_power + epsilon)
    spectra = jnp.einsum("cwn,nm->cwm", normalized, dft_matrix, precision=lax.Precision.HIGHEST)
    return spectra.reshape(row_count, spectra.shape[1], 2, -1).astype(jnp.bfloat16)


def cross_tile(own_spec, other_spec):
    own_real, own_imag = (own_spec[:, :, 0], own_spec[:, :, 1])
    other_real, other_imag = (other_spec[:, :, 0], other_spec[:, :, 1])
    cross_real = jnp.einsum(
        "cwf,kwf->cfk", own_real, other_real, preferred_element_type=jnp.float32
    )
    cross_real = cross_real + jnp.einsum(
        "cwf,kwf->cfk", own_imag, other_imag, preferred_element_type=jnp.float32
    )
    cross_imag = jnp.einsum(
        "cwf,kwf->cfk", own_imag, other_real, preferred_element_type=jnp.float32
    )
    cross_imag = cross_imag - jnp.einsum(
        "cwf,kwf->cfk", own_real, other_imag, preferred_element_type=jnp.float32
    )
    return jnp.concatenate([cross_real, cross_imag], axis=2)


def per_device(strain, fir_taps, spatial):
    taps_now, taps_before = toeplitz_pair(fir_taps)
    dft_matrix = dft_table(BINS, FIRST_BIN, NFFT, fir_taps.dtype)
    rim_width = spatial.shape[0] // 2
    history = strain[:, strain.shape[1] - 128 :]
    earlier = passed_along(history, "rep", 1)
    extended = jnp.concatenate([earlier, strain], axis=1)
    padded = padded_2(extended, (("chan", 0),), rim_width)
    spectra = window_spectra(padded.astype(jnp.float32), spatial, taps_now, taps_before, dft_matrix)
    inverse = 1.0 / (spectra.shape[1] * lax.axis_size("rep"))
    tile_list = [cross_tile(spectra, spectra)]
    partner = spectra
    for offset in range(STEPS):
        partner = from_behind(partner, "chan", -1)
        tile_list.append(cross_tile(spectra, partner))
    partial_tiles = jnp.stack(tile_list, axis=1) * inverse
    cross_tiles = lax.psum_scatter(partial_tiles, "rep", scatter_dimension=2, tiled=True)
    return cross_tiles


def solution(mesh):
    in_specs = (P("chan", "rep"), P(), P())
    out_specs = P("chan", None, "rep", None)
    return jax.shard_map(
        per_device, mesh=mesh, in_specs=in_specs, out_specs=out_specs, check_vma=False
    )
```

profile of v0, /device:TPU:1, one launch (start us, length us, event | category | flops | bytes accessed | tf_op | source)
XLA Modules:
  0.0 177.2 jit_solution(16563687625933781902)
XLA Ops:
  6.5 0.7 slice.110
  7.2 8.8 %collective-permute-start = (bf16[16,128]{1,0:T(8,128)(2,1)S(1)}, bf16[16,128]{1,0:T(8,128)(2,1)S(1)}, u32[]{:S(2)}, u32[]{:S(2)}) collective-permute-start(bf16[16,128]{1,0:T(8,128)(2,1)S(1)} %slice.110), channel_id=1, source_target_pairs={{0,1},{1,2},{2,3},{4,5},{5,6},{6,7},{8,9},{9,10},{10,11},{12,13},{... | collective-permute-start | bytes 12296 | tf_op jit(solution)/shard_map/ppermute | solution.py:20
  16.1 0.6 fusion.43
  16.7 1.7 fusion.45
  18.4 1.3 constant_dynamic-update-slice_fusion
  19.7 0.2 fusion.44
  19.9 2.3 %collective-permute-start.1 = (bf16[4,32896]{1,0:T(4,128)(2,1)S(1)}, bf16[4,32896]{1,0:T(4,128)(2,1)S(1)}, u32[]{:S(2)}, u32[]{:S(2)}) collective-permute-start(bf16[4,32896]{1,0:T(4,128)(2,1)S(1)} %get-tuple-element.7), channel_id=1, source_target_pairs={{0,4},{4,8},{8,12},{12,16},{16,20},{20,24},{24,28},{28,32},{32,36}... | collective-permute-start | bytes 789512 | tf_op jit(solution)/shard_map/ppermute | solution.py:31
  22.3 1.3 collective-permute-start.2
  23.6 0.8 select_reduce_fusion.1
  24.4 2.4 %collective-permute-done.1 = bf16[4,32896]{1,0:T(4,128)(2,1)S(1)} collective-permute-done((bf16[4,32896]{1,0:T(4,128)(2,1)S(1)}, bf16[4,32896]{1,0:T(4,128)(2,1)S(1)}, u32[]{:S(2)}, u32[]{:S(2)}) %collective-permute-start.1) | collective-permute-done | bytes 263200 | tf_op jit(solution)/shard_map/ppermute | solution.py:31
  26.8 6.9 %collective-permute-done.2 = bf16[4,32896]{1,0:T(4,128)(2,1)S(1)} collective-permute-done((bf16[4,32896]{1,0:T(4,128)(2,1)S(1)}, bf16[4,32896]{1,0:T(4,128)(2,1)S(1)}, u32[]{:S(2)}, u32[]{:S(2)}) %collective-permute-start.2) | collective-permute-done | bytes 263200 | tf_op jit(solution)/shard_map/ppermute | solution.py:33
  33.8 0.6 maximum_convert_fusion
  34.3 8.7 %fusion = f32[16,32896]{1,0:T(8,128)} fusion(f32[24,32896]{1,0:T(8,128)S(1)} %maximum_convert_fusion, f32[]{:T(128)} %bitcast.8, f32[]{:T(128)} %bitcast.7, f32[]{:T(128)} %bitcast.6, f32[]{:T(128)} %bitcast.5, f32[]{:T(128)} %bitcast.4, f32[]{:T(128)} %bitcast.3, f32[]{:T(128)} %bitcast.2, f32[]{:T(128)} %bitcast.1, f32[]{:T(128)} %bitcast), kind=kLoop, calls=%fused_computation.5 | loop fusion | flops 8947712 | bytes 21053476 | tf_op jit(solution)/shard_map/add | solution.py:72
  43.1 1.7 reshape.57
  44.8 2.0 %fusion.8 = f32[16,256,128]{1,2,0:T(8,128)S(1)} fusion(f32[16,257,128]{2,1,0:T(8,128)S(1)} %reshape.57, f32[128,128]{1,0:T(8,128)S(1)} %get-tuple-element.6), kind=kOutput, calls=%fused_computation.21 | convolution fusion | flops 805306368 | bytes 4259840 | tf_op jit(solution)/shard_map/cbj,ji->cbi/dot_general | solution.py:77
  46.8 3.7 %multiply_reduce_fusion = (f32[16,256]{1,0:T(8,128)S(1)}, f32[16,256,128]{1,2,0:T(8,128)}) fusion(f32[16,256,128]{1,2,0:T(8,128)S(1)} %fusion.8, f32[128,128]{1,0:T(8,128)S(1)} %get-tuple-element.5, f32[16,257,128]{2,1,0:T(8,128)S(1)} %reshape.57), kind=kOutput, calls=%fused_computation.27 | convolution fusion | flops 806875136 | bytes 6373376 | tf_op jit(solution)/shard_map/cbj,ji->cbi/dot_general | solution.py:74
  50.8 1.9 %broadcast_divide_fusion = f32[16,256,128]{1,2,0:T(8,128)S(1)} fusion(f32[16,256,128]{1,2,0:T(8,128)} %get-tuple-element.31, f32[16,256]{1,0:T(8,128)S(1)} %copy.135), kind=kLoop, calls=%fused_computation.52 | loop fusion | flops 524288 | bytes 4210688 | tf_op jit(solution)/shard_map/div | solution.py:82
  52.6 1.9 %copy.136 = f32[16,256,128]{2,1,0:T(8,128)} copy(f32[16,256,128]{1,2,0:T(8,128)S(1)} %broadcast_divide_fusion) | data formatting | bytes 4194304 | tf_op jit(solution)/shard_map/div | solution.py:82
  54.5 1.7 reshape.60
  56.2 1.8 %fusion.17 = bf16[16,32,2,32]{3,1,2,0:T(8,128)(2,1)S(1)} fusion(f32[2,32,1024,1]{2,1,0,3:T(8,128)S(1)} %bitcast.140, f32[16,32,1024,1]{2,1,0,3:T(8,128)S(1)} %reshape.60), kind=kOutput, calls=%fused_computation.31 | convolution fusion | flops 402685952 | bytes 2424832 | tf_op jit(solution)/shard_map/cwn,nm->cwm/dot_general | solution.py:83
  58.0 8.8 %collective-permute-start.3 = (bf16[16,32,2,32]{3,1,2,0:T(8,128)(2,1)S(1)}, bf16[16,32,2,32]{3,1,2,0:T(8,128)(2,1)S(1)}, u32[]{:S(2)}, u32[]{:S(2)}) collective-permute-start(bf16[16,32,2,32]{3,1,2,0:T(8,128)(2,1)S(1)} %fusion.17), channel_id=1, source_target_pairs={{4,0},{8,4},{12,8},{16,12},{20,16},{24,20},{28,24},{32,28},{36,32}... | collective-permute-start | bytes 196616 | tf_op jit(solution)/shard_map/ppermute | solution.py:43
  67.4 0.2 fusion.47
  67.6 0.2 fusion.29
  67.9 0.2 fusion.28
  68.2 3.2 %collective-permute-done.3 = bf16[16,32,2,32]{3,1,2,0:T(8,128)(2,1)S(1)} collective-permute-done((bf16[16,32,2,32]{3,1,2,0:T(8,128)(2,1)S(1)}, bf16[16,32,2,32]{3,1,2,0:T(8,128)(2,1)S(1)}, u32[]{:S(2)}, u32[]{:S(2)}) %collective-permute-start.3) | collective-permute-done | bytes 65568 | tf_op jit(solution)/shard_map/ppermute | solution.py:43
  71.6 0.2 fusion.48
  71.8 0.2 fusion.49
  72.2 0.2 fusion.27
  72.4 0.2 fusion.26
  72.6 9.8 %collective-permute-start.4 = (bf16[16,32,2,32]{3,1,2,0:T(8,128)(2,1)S(1)}, bf16[16,32,2,32]{3,1,2,0:T(8,128)(2,1)S(1)}, u32[]{:S(2)}, u32[]{:S(2)}) collective-permute-start(bf16[16,32,2,32]{3,1,2,0:T(8,128)(2,1)S(1)} %collective-permute-done.3), channel_id=1, source_target_pairs={{4,0},{8,4},{12,8},{16,12},{20,16},{24,20},{28,24},{32,28},{36,32}... | collective-permute-start | bytes 196616 | tf_op jit(solution)/shard_map/ppermute | solution.py:43
  82.6 5.8 %collective-permute-done.4 = bf16[16,32,2,32]{3,1,2,0:T(8,128)(2,1)S(1)} collective-permute-done((bf16[16,32,2,32]{3,1,2,0:T(8,128)(2,1)S(1)}, bf16[16,32,2,32]{3,1,2,0:T(8,128)(2,1)S(1)}, u32[]{:S(2)}, u32[]{:S(2)}) %collective-permute-start.4) | collective-permute-done | bytes 65568 | tf_op jit(solution)/shard_map/ppermute | solution.py:43
  88.8 0.2 fusion.51
  89.2 0.2 fusion.25
  89.4 0.2 fusion.24
  89.6 9.9 %collective-permute-start.5 = (bf16[16,32,2,32]{3,1,2,0:T(8,128)(2,1)S(1)}, bf16[16,32,2,32]{3,1,2,0:T(8,128)(2,1)S(1)}, u32[]{:S(2)}, u32[]{:S(2)}) collective-permute-start(bf16[16,32,2,32]{3,1,2,0:T(8,128)(2,1)S(1)} %collective-permute-done.4), channel_id=1, source_target_pairs={{4,0},{8,4},{12,8},{16,12},{20,16},{24,20},{28,24},{32,28},{36,32}... | collective-permute-start | bytes 196616 | tf_op jit(solution)/shard_map/ppermute | solution.py:43
  99.7 5.1 %collective-permute-done.5 = bf16[16,32,2,32]{3,1,2,0:T(8,128)(2,1)S(1)} collective-permute-done((bf16[16,32,2,32]{3,1,2,0:T(8,128)(2,1)S(1)}, bf16[16,32,2,32]{3,1,2,0:T(8,128)(2,1)S(1)}, u32[]{:S(2)}, u32[]{:S(2)}) %collective-permute-start.5) | collective-permute-done | bytes 65568 | tf_op jit(solution)/shard_map/ppermute | solution.py:43
  105.2 0.2 fusion.53
  105.6 0.2 fusion.23
  105.8 0.2 fusion.22
  106.0 10.1 %collective-permute-start.6 = (bf16[16,32,2,32]{3,1,2,0:T(8,128)(2,1)S(1)}, bf16[16,32,2,32]{3,1,2,0:T(8,128)(2,1)S(1)}, u32[]{:S(2)}, u32[]{:S(2)}) collective-permute-start(bf16[16,32,2,32]{3,1,2,0:T(8,128)(2,1)S(1)} %collective-permute-done.5), channel_id=1, source_target_pairs={{4,0},{8,4},{12,8},{16,12},{20,16},{24,20},{28,24},{32,28},{36,32}... | collective-permute-start | bytes 196616 | tf_op jit(solution)/shard_map/ppermute | solution.py:43
  116.2 4.2 %collective-permute-done.6 = bf16[16,32,2,32]{3,1,2,0:T(8,128)(2,1)S(1)} collective-permute-done((bf16[16,32,2,32]{3,1,2,0:T(8,128)(2,1)S(1)}, bf16[16,32,2,32]{3,1,2,0:T(8,128)(2,1)S(1)}, u32[]{:S(2)}, u32[]{:S(2)}) %collective-permute-start.6) | collective-permute-done | bytes 65568 | tf_op jit(solution)/shard_map/ppermute | solution.py:43
  120.9 0.2 fusion.55
  121.3 0.2 fusion.21
  121.5 0.2 fusion.20
  121.9 1.2 reshape.63
  123.2 45.4 %reduce-scatter.4.cloned.1.call-done = f32[8,2560]{1,0:T(8,128)} async-done(((f32[32,2560]{1,0:T(8,128)}), f32[8,2560]{1,0:T(8,128)}) %reduce-scatter.4.cloned.1.call-update) | async-done | bytes 81936
  168.5 1.0 reshape.64
  169.6 0.8 copy.177
  (40 shorter events, 3.7 us)
Async XLA Ops:
  6.5 17.0 %copy-start = (f32[60]{0:T(128)S(1)}, f32[60]{0:T(128)}, u32[]{:S(2)}) copy-start(f32[60]{0:T(128)} %param.4) | copy-start | bytes 724
  6.5 162.0 %reduce-scatter.4.cloned.1.call-start = ((), (), s32[]{:S(2)}) async-start(), calls=%async_computation.1 | async-start | bytes 409600
  7.2 11.2 %collective-permute-start = (bf16[16,128]{1,0:T(8,128)(2,1)S(1)}, bf16[16,128]{1,0:T(8,128)(2,1)S(1)}, u32[]{:S(2)}, u32[]{:S(2)}) collective-permute-start(bf16[16,128]{1,0:T(8,128)(2,1)S(1)} %slice.110), channel_id=1, source_target_pairs={{0,1},{1,2},{2,3},{4,5},{5,6},{6,7},{8,9},{9,10},{10,11},{12,13},{... | collective-permute-start | bytes 12296 | tf_op jit(solution)/shard_map/ppermute | solution.py:20
  19.9 6.9 %collective-permute-start.1 = (bf16[4,32896]{1,0:T(4,128)(2,1)S(1)}, bf16[4,32896]{1,0:T(4,128)(2,1)S(1)}, u32[]{:S(2)}, u32[]{:S(2)}) collective-permute-start(bf16[4,32896]{1,0:T(4,128)(2,1)S(1)} %get-tuple-element.7), channel_id=1, source_target_pairs={{0,4},{4,8},{8,12},{12,16},{16,20},{20,24},{24,28},{28,32},{32,36}... | collective-permute-start | bytes 789512 | tf_op jit(solution)/shard_map/ppermute | solution.py:31
  22.3 11.5 %collective-permute-start.2 = (bf16[4,32896]{1,0:T(4,128)(2,1)S(1)}, bf16[4,32896]{1,0:T(4,128)(2,1)S(1)}, u32[]{:S(2)}, u32[]{:S(2)}) collective-permute-start(bf16[4,32896]{1,0:T(4,128)(2,1)S(1)} %get-tuple-element.8), channel_id=1, source_target_pairs={{4,0},{8,4},{12,8},{16,12},{20,16},{24,20},{28,24},{32,28},{36,32}... | collective-permute-start | bytes 789512 | tf_op jit(solution)/shard_map/ppermute | solution.py:33
  58.0 13.4 %collective-permute-start.3 = (bf16[16,32,2,32]{3,1,2,0:T(8,128)(2,1)S(1)}, bf16[16,32,2,32]{3,1,2,0:T(8,128)(2,1)S(1)}, u32[]{:S(2)}, u32[]{:S(2)}) collective-permute-start(bf16[16,32,2,32]{3,1,2,0:T(8,128)(2,1)S(1)} %fusion.17), channel_id=1, source_target_pairs={{4,0},{8,4},{12,8},{16,12},{20,16},{24,20},{28,24},{32,28},{36,32}... | collective-permute-start | bytes 196616 | tf_op jit(solution)/shard_map/ppermute | solution.py:43
  72.6 15.8 %collective-permute-start.4 = (bf16[16,32,2,32]{3,1,2,0:T(8,128)(2,1)S(1)}, bf16[16,32,2,32]{3,1,2,0:T(8,128)(2,1)S(1)}, u32[]{:S(2)}, u32[]{:S(2)}) collective-permute-start(bf16[16,32,2,32]{3,1,2,0:T(8,128)(2,1)S(1)} %collective-permute-done.3), channel_id=1, source_target_pairs={{4,0},{8,4},{12,8},{16,12},{20,16},{24,20},{28,24},{32,28},{36,32}... | collective-permute-start | bytes 196616 | tf_op jit(solution)/shard_map/ppermute | solution.py:43
  89.6 15.2 %collective-permute-start.5 = (bf16[16,32,2,32]{3,1,2,0:T(8,128)(2,1)S(1)}, bf16[16,32,2,32]{3,1,2,0:T(8,128)(2,1)S(1)}, u32[]{:S(2)}, u32[]{:S(2)}) collective-permute-start(bf16[16,32,2,32]{3,1,2,0:T(8,128)(2,1)S(1)} %collective-permute-done.4), channel_id=1, source_target_pairs={{4,0},{8,4},{12,8},{16,12},{20,16},{24,20},{28,24},{32,28},{36,32}... | collective-permute-start | bytes 196616 | tf_op jit(solution)/shard_map/ppermute | solution.py:43
  106.0 14.5 %collective-permute-start.6 = (bf16[16,32,2,32]{3,1,2,0:T(8,128)(2,1)S(1)}, bf16[16,32,2,32]{3,1,2,0:T(8,128)(2,1)S(1)}, u32[]{:S(2)}, u32[]{:S(2)}) collective-permute-start(bf16[16,32,2,32]{3,1,2,0:T(8,128)(2,1)S(1)} %collective-permute-done.5), channel_id=1, source_target_pairs={{4,0},{8,4},{12,8},{16,12},{20,16},{24,20},{28,24},{32,28},{36,32}... | collective-permute-start | bytes 196616 | tf_op jit(solution)/shard_map/ppermute | solution.py:43
Sparse Core Ops, SparseCore 0:
  123.3 45.2 reduce-scatter.3
where the time goes:
time: 178 us; the launch traced here: 177 us
  waiting for transfers between devices  73.1 us (41%)
  starting transfers between devices  51.1 us (29%)
  local copies, waits for them, and re-layouts  14.2 us (8%)
  between operations  13.8 us (8%)
  other arithmetic  13.4 us (8%)
  matrix products  11.5 us (6%)
    unnamed x2, waiting for transfers between devices  45.4 us
    ppermute x4, starting transfers between devices, from_behind(): return lax.ppermute(block, axis, route)  38.7 us
    ppermute x4, waiting for transfers between devices, from_behind(): return lax.ppermute(block, axis, route)  18.4 us
    ppermute x1, starting transfers between devices, passed_along(): return lax.ppermute(shard, axis, pairs)  8.82 us
    add x1, other arithmetic, window_spectra(): mixed_rows + spatial[offset] * channel_rows[offset:offset + row_count]  8.72 us
    ppermute x1, waiting for transfers between devices, padded_2(): lax.ppermute(head, axis, [((i + 1) % count, i) for i in range(ends)])  6.93 us
    dot_general x1, matrix products, window_spectra(): jnp.einsum('cbj,ji->cbi', time_blocks[:, 1:], taps_now, precision=lax.Pre...  3.72 us
    div x4, local copies, waits for them, and re-layouts, window_spectra(): normalized = window_data / jnp.sqrt(window_power + epsilon)  3.65 us
  transfers between devices with their start and end apart: 8, of which 7 were waited for; matrix products, arithmetic and copies ran while one was open for 3% of the time, Pallas kernels for 0%

commit v1 on v0

v1 whole, which is shorter than its diff:
```python
import functools
import math

import jax
import jax.numpy as jnp
import ml_dtypes
import numpy as np
from jax import lax
from jax.experimental import pallas as pl
from jax.experimental.pallas import tpu as pltpu
from jax.sharding import PartitionSpec as P

NFFT = 1024
BINS = 32
FIRST_BIN = 16
EPSILON = 1e-05
LANES = 128
CW = 8
GROUP = 8
BLOCKS_PER_WINDOW = NFFT // LANES
MESH = pl.DeviceIdType.MESH
F32 = jnp.float32
BF16 = jnp.bfloat16


def split_table(values):
    high = values.astype(ml_dtypes.bfloat16)
    low = (values - high.astype(np.float64)).astype(ml_dtypes.bfloat16)
    return high, low


def tables():
    sample = np.arange(LANES)[:, None, None]
    block = np.arange(BLOCKS_PER_WINDOW)[None, :, None]
    bins = (FIRST_BIN + np.arange(BINS))[None, None, :]
    angle = ((block * LANES + sample) * bins % NFFT) * (2.0 * math.pi / NFFT)
    parts = np.concatenate([np.cos(angle), -np.sin(angle)], axis=2) / math.sqrt(NFFT)
    parts = np.concatenate([parts, np.zeros_like(parts)], axis=2)
    high, low = split_table(parts.reshape(LANES, BLOCKS_PER_WINDOW * LANES))
    row = np.arange(2 * BINS)[:, None]
    lane = np.arange(1024)[None, :]
    source = (lane // 512) * BINS + (lane % 512) // LANES * GROUP + lane % GROUP
    choose = (row == source).astype(ml_dtypes.bfloat16)
    return np.concatenate([high, low, choose], axis=0)


def iota(shape, dim):
    return lax.broadcasted_iota(jnp.int32, shape, dim)


def dot(a, b):
    return jnp.dot(a, b, preferred_element_type=F32)


def kernel(
    chans, reps, strain, taps, spatial, table, out,
    own, rim, fir_w, fold_w, tab, filt, raw, power_low, own_raw, packs, gathered, tiles,
    local_sem, rim_send, rim_recv, hist_send, hist_recv, one_send, one_recv, two_send, two_recv,
):
    b = lax.axis_index("chan")
    r = lax.axis_index("rep")
    samples = strain.shape[1]
    windows = samples // NFFT
    chunks = windows // CW
    span = CW * NFFT

    def block_at(step):
        return lax.rem(b + (step + chans), chans)

    def rep_at(step):
        return lax.rem(r + (step + reps), reps)

    barrier = pltpu.get_barrier_semaphore()
    peers = [(s, 0) for s in (-4, -3, -2, -1, 1, 2, 3, 4)] + [(0, d) for d in range(1, reps)] + [(-1, 1), (1, -1)]
    for s, d in peers:
        pl.semaphore_signal(
            barrier, inc=1, device_id={"chan": block_at(s), "rep": rep_at(d)}, device_id_type=MESH
        )
    fetch_own = pltpu.make_async_copy(strain, own.at[:, pl.ds(LANES, samples)], local_sem.at[0])
    fetch_own.start()
    fetch_tab = pltpu.make_async_copy(table, tab, local_sem.at[1])
    fetch_tab.start()

    row, lane = iota((LANES, LANES), 0), iota((LANES, LANES), 1)
    tap_row = jnp.concatenate([taps[...], jnp.zeros((1, LANES - taps.shape[1]), F32)], axis=1)
    circulant = pltpu.roll(jnp.broadcast_to(tap_row, (LANES, LANES)), 0, 1, stride=1, stride_axis=0)
    now = jnp.where(lane >= row, circulant, 0.0)
    before = jnp.where(lane < row, circulant, 0.0)
    both = jnp.concatenate([before, now], axis=0)
    both_high = both.astype(BF16)
    both_low = (both - both_high.astype(F32)).astype(BF16)
    fir_w[:, 0:LANES] = both_high
    fir_w[:, LANES:] = both_low
    fetch_tab.wait()
    folded = dot(
        jnp.concatenate([both_high, both_low, both_high], axis=1),
        jnp.concatenate([tab[0:LANES], tab[0:LANES], tab[LANES : 2 * LANES]], axis=0),
    )
    for q in range(BLOCKS_PER_WINDOW + 1):
        part = jnp.zeros((LANES, LANES), F32)
        if q > 0:
            part = part + folded[LANES:, (q - 1) * LANES : q * LANES]
        if q < BLOCKS_PER_WINDOW:
            part = part + folded[0:LANES, q * LANES : (q + 1) * LANES]
        part_high = part.astype(BF16)
        fold_w[q * LANES : (q + 1) * LANES, 0:LANES] = part_high
        fold_w[q * LANES : (q + 1) * LANES, LANES:] = (part - part_high.astype(F32)).astype(BF16)

    half_row = iota((8, LANES), 0)
    weights = [spatial[j] for j in range(9)]
    crossing = []
    for j in range(9):
        same = (half_row < 4) == (half_row + (8 + j) < 16)
        keep = jnp.logical_or(same, b != chans - 1)
        crossing.append(jnp.where(keep, weights[j], 0.0))

    pl.semaphore_wait(barrier, len(peers))

    rim_copies = []
    for k in range(chunks):
        if k == 0:
            source = strain.at[pl.ds(0, 8), pl.ds(0, span)]
            target = rim.at[k, :, pl.ds(LANES, span)]
        else:
            source = strain.at[pl.ds(0, 8), pl.ds(k * span - LANES, span + LANES)]
            target = rim.at[k]
        rim_copies.append(
            pltpu.make_async_remote_copy(
                source, target, rim_send.at[k], rim_recv.at[k],
                device_id={"chan": block_at(-1), "rep": r}, device_id_type=MESH,
            )
        )
    hist_own = pltpu.make_async_remote_copy(
        strain.at[:, pl.ds(samples - LANES, LANES)], own.at[:, pl.ds(0, LANES)],
        hist_send.at[0], hist_recv.at[0],
        device_id={"chan": b, "rep": rep_at(1)}, device_id_type=MESH,
    )
    hist_rim = pltpu.make_async_remote_copy(
        strain.at[pl.ds(0, 8), pl.ds(samples - LANES, LANES)], rim.at[0, :, pl.ds(0, LANES)],
        hist_send.at[1], hist_recv.at[1],
        device_id={"chan": block_at(-1), "rep": rep_at(1)}, device_id_type=MESH,
    )
    hist_own.start()
    hist_rim.start()
    for k in reversed(range(chunks)):
        rim_copies[k].start()
    fetch_own.wait()

    def lower_window(w):
        base = pl.multiple_of(w * NFFT, LANES)
        left = jnp.concatenate([own[:, pl.ds(base + i * LANES, 2 * LANES)] for i in range(BLOCKS_PER_WINDOW)], axis=0)
        both_parts = dot(left, fir_w[...])
        band = both_parts[:, 0:LANES] + both_parts[:, LANES:]
        for i in range(BLOCKS_PER_WINDOW):
            filt[w, i * 24 : i * 24 + 16, :] = band[i * 16 : i * 16 + 16]
        squares = jnp.zeros((8, LANES), F32)
        for i in range(BLOCKS_PER_WINDOW):
            mixed = weights[0] * filt[w, i * 24 : i * 24 + 8, :]
            for j in range(1, 9):
                mixed = mixed + weights[j] * filt[w, i * 24 + j : i * 24 + j + 8, :]
            squares = squares + mixed * mixed
        power_low[w] = squares

    def lower_chunk(k):
        first = k * CW

        def body(t, carry):
            lower_window(first + t)
            return carry

        lax.fori_loop(0, CW, body, 0)
        left = jnp.concatenate(
            [own[:, pl.ds((first + t) * NFFT, NFFT + LANES)] for t in range(CW)], axis=0
        )
        parts = dot(left, fold_w[...])
        own_raw[k] = parts[:, 0:LANES] + parts[:, LANES:]

    def upper_chunk(k):
        first = k * CW

        def body(t, carry):
            w = first + t
            base = pl.multiple_of(t * NFFT, LANES)
            left = jnp.concatenate(
                [rim[k, :, pl.ds(base + i * LANES, 2 * LANES)] for i in range(BLOCKS_PER_WINDOW)], axis=0
            )
            both_parts = dot(left, fir_w[...])
            band = both_parts[:, 0:LANES] + both_parts[:, LANES:]
            for i in range(BLOCKS_PER_WINDOW):
                filt[w, i * 24 + 16 : i * 24 + 24, :] = band[i * 8 : i * 8 + 8]
            squares = jnp.zeros((8, LANES), F32)
            for i in range(BLOCKS_PER_WINDOW):
                mixed = crossing[0] * filt[w, i * 24 + 8 : i * 24 + 16, :]
                for j in range(1, 9):
                    mixed = mixed + crossing[j] * filt[w, i * 24 + 8 + j : i * 24 + 16 + j, :]
                squares = squares + mixed * mixed
            raw[t, 24:32, :] = squares
            return carry

        lax.fori_loop(0, CW, body, 0)
        left = jnp.concatenate([rim[k, :, pl.ds(t * NFFT, NFFT + LANES)] for t in range(CW)], axis=0)
        parts = dot(left, fold_w[...])
        rim_raw = parts[:, 0:LANES] + parts[:, LANES:]
        pieces = []
        for t in range(CW):
            raw[t, 0:16, :] = own_raw[k, t * 16 : t * 16 + 16, :]
            raw[t, 16:24, :] = rim_raw[t * 8 : t * 8 + 8]
            lower = weights[0] * raw[t, 0:8, :]
            upper = crossing[0] * raw[t, 8:16, :]
            for j in range(1, 9):
                lower = lower + weights[j] * raw[t, j : j + 8, :]
                upper = upper + crossing[j] * raw[t, 8 + j : 16 + j, :]
            for value, squares in ((lower, power_low[first + t]), (upper, raw[t, 24:32, :])):
                mean = jnp.sum(squares, axis=1, keepdims=True) * (1.0 / NFFT)
                pieces.append(value / jnp.sqrt(mean + EPSILON))
        spectra = jnp.concatenate(pieces, axis=0).astype(BF16)
        spread = dot(spectra[:, 0 : 2 * BINS], tab[2 * LANES : 2 * LANES + 2 * BINS])
        rows, lanes = iota((LANES, LANES), 0), iota((LANES, LANES), 1)
        mine = lax.rem(lax.rem(rows, 16) + 4, 16) == lanes // GROUP
        columns = [
            jnp.where(mine, spread[:, g * LANES : (g + 1) * LANES], 0.0).astype(BF16) for g in range(8)
        ]
        stacked = jnp.concatenate(
            [jnp.concatenate(columns[0:4], axis=1), jnp.concatenate(columns[4:8], axis=1)], axis=0
        )
        collect = jnp.where(
            iota((16, 256), 0) == iota((16, 256), 1) // 16, 1.0, 0.0
        ).astype(BF16)
        packed = dot(collect, stacked).astype(BF16)
        for g in range(reps):
            packs[k, g] = packed[:, g * LANES : (g + 1) * LANES]
        gathered[1, k, r] = packs[k, r]

    def first_copy(k, d):
        return pltpu.make_async_remote_copy(
            packs.at[k, rep_at(d)], gathered.at[1, k, r], one_send.at[k, d - 1], one_recv.at[k, d - 1],
            device_id={"chan": b, "rep": rep_at(d)}, device_id_type=MESH,
        )

    def second_copy(k, s):
        slot = 0 if s == 0 else s + 1
        return pltpu.make_async_remote_copy(
            gathered.at[1, k], gathered.at[slot, k], two_send.at[k, s], two_recv.at[k, s],
            device_id={"chan": block_at(1 if s == 0 else -s), "rep": r}, device_id_type=MESH,
        )

    order = list(reversed(range(chunks)))
    for k in order:
        if k == 0:
            hist_own.wait_recv()

            @pl.when(r == 0)
            def _():
                own[:, 0:LANES] = jnp.zeros((16, LANES), BF16)

        lower_chunk(k)

    def forward(k):
        for d in range(1, reps):
            first_copy(k, d).wait_recv()
        for s in range(5):
            second_copy(k, s).start()

    for place, k in enumerate(order):
        rim_copies[k].wait_recv()
        if k == 0:
            hist_rim.wait_recv()

            @pl.when(r == 0)
            def _():
                rim[0, :, 0:LANES] = jnp.zeros((8, LANES), BF16)

        upper_chunk(k)
        for d in range(1, reps):
            first_copy(k, d).start()
        if place > 0:
            forward(order[place - 1])
    forward(order[-1])
    for k in order:
        for s in range(5):
            second_copy(k, s).wait_recv()

    depth = chunks * reps * 16
    own_lanes = iota((depth, LANES), 1) < 32

    def merged(s):
        return jnp.where(
            own_lanes,
            gathered[s].reshape(depth, LANES).astype(F32),
            gathered[s + 1].reshape(depth, LANES).astype(F32),
        )

    mine = merged(0)
    cubes = mine.reshape(chunks * reps, 2, 8, LANES)
    swapped = jnp.concatenate([cubes[:, 1:2], -cubes[:, 0:1]], axis=1).reshape(depth, LANES)
    left = jnp.concatenate([mine.T, swapped.T], axis=0).astype(BF16)
    same_bin = lax.rem(iota((LANES, LANES), 0), GROUP) == lax.rem(iota((LANES, LANES), 1), GROUP)
    pick_row, pick_lane = iota((LANES, LANES), 0), iota((LANES, LANES), 1)
    pick_real = jnp.where(pick_lane == pick_row // GROUP, 1.0, 0.0).astype(BF16)
    pick_imag = jnp.where(pick_lane == 16 + pick_row // GROUP, 1.0, 0.0).astype(BF16)
    picks = jnp.concatenate([pick_real, pick_imag] * 3, axis=0)
    scale = 1.0 / (windows * reps)
    for s in range(5):
        block = (mine if s == 0 else merged(s)).astype(BF16)
        product = dot(left, block)
        real = jnp.where(same_bin, product[0:LANES], 0.0) * scale
        imag = jnp.where(same_bin, product[LANES:], 0.0) * scale
        terms = []
        for _ in range(3):
            real_part, imag_part = real.astype(BF16), imag.astype(BF16)
            terms += [real_part, imag_part]
            real, imag = real - real_part.astype(F32), imag - imag_part.astype(F32)
        tile = dot(jnp.concatenate(terms, axis=1), picks)
        for c in range(16):
            out[c, s] = tile[c * GROUP : (c + 1) * GROUP, 0:32]

    for k in range(chunks):
        rim_copies[k].wait_send()
        for d in range(1, reps):
            first_copy(k, d).wait_send()
        for s in range(5):
            second_copy(k, s).wait_send()
    hist_own.wait_send()
    hist_rim.wait_send()


def solution(mesh):
    chans, reps = mesh.shape["chan"], mesh.shape["rep"]

    def per_device(strain, fir_taps, spatial):
        rows, samples = strain.shape
        windows = samples // NFFT
        chunks = windows // CW
        span = CW * NFFT
        anywhere = pl.BlockSpec(memory_space=pl.ANY)
        vmem = pl.BlockSpec(memory_space=pltpu.VMEM)
        return pl.pallas_call(
            functools.partial(kernel, chans, reps),
            out_shape=jax.ShapeDtypeStruct((rows, 5, BINS // reps, 32), F32),
            in_specs=[anywhere, vmem, pl.BlockSpec(memory_space=pltpu.SMEM), anywhere],
            out_specs=vmem,
            scratch_shapes=[
                pltpu.VMEM((rows, samples + LANES), BF16),
                pltpu.VMEM((chunks, 8, span + LANES), BF16),
                pltpu.VMEM((2 * LANES, 2 * LANES), BF16),
                pltpu.VMEM((NFFT + LANES, 2 * LANES), BF16),
                pltpu.VMEM((2 * LANES + 2 * BINS, 1024), BF16),
                pltpu.VMEM((windows, 192, LANES), F32),
                pltpu.VMEM((CW, 32, LANES), F32),
                pltpu.VMEM((windows, 8, LANES), F32),
                pltpu.VMEM((chunks, CW * 16, LANES), F32),
                pltpu.VMEM((chunks, reps, 16, LANES), BF16),
                pltpu.VMEM((6, chunks, reps, 16, LANES), BF16),
                pltpu.VMEM((8, LANES), F32),
                pltpu.SemaphoreType.DMA((2,)),
                pltpu.SemaphoreType.DMA((chunks,)),
                pltpu.SemaphoreType.DMA((chunks,)),
                pltpu.SemaphoreType.DMA((2,)),
                pltpu.SemaphoreType.DMA((2,)),
                pltpu.SemaphoreType.DMA((chunks, 3)),
                pltpu.SemaphoreType.DMA((chunks, 3)),
                pltpu.SemaphoreType.DMA((chunks, 5)),
                pltpu.SemaphoreType.DMA((chunks, 5)),
            ],
            compiler_params=pltpu.CompilerParams(
                collective_id=0, has_side_effects=True, vmem_limit_bytes=40 * 1024 * 1024
            ),
        )(strain, fir_taps.reshape(1, -1), spatial, jnp.asarray(tables()))

    return jax.shard_map(
        per_device,
        mesh=mesh,
        in_specs=(P("chan", "rep"), P(), P()),
        out_specs=P("chan", None, "rep", None),
        check_vma=False,
    )
```

time: 178 us -> 52.4 us (0.29)
  waiting for transfers between devices: 73.1 us -> 0 us
  starting transfers between devices: 51.1 us -> 0 us
  Pallas kernels: 0 us -> 48.5 us
  between operations: 13.8 us -> 0.01 us
  other arithmetic: 13.4 us -> 0 us
  matrix products: 11.5 us -> 0 us
  local copies, waits for them, and re-layouts: 14.2 us -> 3.71 us
    ppermute x7 -> x0, starting transfers between devices: 51.1 us -> none  [the longest x4 38.7 us: from_behind(): return lax.ppermute(block, axis, route)]
    pallas_call x0 -> x1, Pallas kernels: none -> 48.5 us  [per_device(): pl.pallas_call(functools.partial(kernel, chans, reps), out_shape=jax.Shap...]
    unnamed x2 -> x0, waiting for transfers between devices: 45.4 us -> none
    ppermute x7 -> x0, waiting for transfers between devices: 27.7 us -> none  [the longest x4 18.4 us: from_behind(): return lax.ppermute(block, axis, route)]
    dot_general x23 -> x0, matrix products: 11.5 us -> none  [the longest x1 3.72 us: window_spectra(): jnp.einsum('cbj,ji->cbi', time_blocks[:, 1:], taps_now, precision=lax.Pre...]
    add x3 -> x0, other arithmetic: 8.73 us -> none  [the longest x1 8.72 us: window_spectra(): mixed_rows + spatial[offset] * channel_rows[offset:offset + row_count]]
    div x4 -> x0, local copies, waits for them, and re-layouts: 3.65 us -> none  [window_spectra(): normalized = window_data / jnp.sqrt(window_power + epsilon)]
    slice x3 -> x0, local copies, waits for them, and re-layouts: 2.56 us -> none  [the longest x1 1.66 us: window_spectra(): mixed_rows = spatial[0] * channel_rows[0:row_count]]
  transfers between devices with their start and end apart: 8 -> 0, of which waited for: 7 -> 0; matrix products, arithmetic and copies ran while one was open for 3% -> 0% of each run, Pallas kernels for 0% -> 0%
where the time goes in v1:
time: 52.4 us; the launch traced here: 52.2 us
  Pallas kernels  48.5 us (93%)
  local copies, waits for them, and re-layouts  3.71 us (7%)
    pallas_call x1, Pallas kernels, per_device(): pl.pallas_call(functools.partial(kernel, chans, reps), out_shape=jax.Shap...  48.5 us
    unnamed x9, local copies, waits for them, and re-layouts  3.71 us

profile of v1, /device:TPU:1, one launch (start us, length us, event | category | flops | bytes accessed | tf_op | source)
XLA Modules:
  0.0 52.2 jit_solution(2494031063829874361)
XLA Ops:
  0.0 0.0 copy-start.3
  0.0 0.0 copy-start.2
  0.0 0.7 %copy-done.3 = f32[9]{0:T(128)S(1)} copy-done((f32[9]{0:T(128)S(1)}, f32[9]{0:T(128)}, u32[]{:S(2)}) %copy-start.3) | copy-done | bytes 60
  0.7 0.0 copy-done.2
  0.7 0.0 copy-start
  0.7 1.2 %copy-done = bf16[16,32768]{1,0:T(8,128)(2,1)S(1)} copy-done((bf16[16,32768]{1,0:T(8,128)(2,1)S(1)}, bf16[16,32768]{1,0:T(8,128)(2,1)}, u32[]{:S(2)}) %copy-start) | copy-done | bytes 1048600
  1.9 0.0 copy-start.1
  1.9 1.1 %copy-done.1 = bf16[320,1024]{1,0:T(8,128)(2,1)S(1)} copy-done((bf16[320,1024]{1,0:T(8,128)(2,1)S(1)}, bf16[320,1024]{1,0:T(8,128)(2,1)}, u32[]{:S(2)}) %copy-start.1) | copy-done | bytes 655384
  3.0 48.5 %shard_map.46 = f32[16,5,8,32]{3,2,1,0:T(8,128)S(1)} custom-call(bf16[16,32768]{1,0:T(8,128)(2,1)S(1)} %copy-done, f32[1,60]{1,0:T(1,128)S(1)} %bitcast.1, f32[9]{0:T(128)S(1)} %copy-done.3, bf16[320,1024]{1,0:T(8,128)(2,1)S(1)} %copy-done.1), custom_call_target="tpu_custom_call" | custom-call | tf_op jit(solution)/shard_map/pallas_call | solution.py:337
  51.5 0.7 %copy.6 = f32[16,5,8,32]{3,2,1,0:T(8,128)} copy(f32[16,5,8,32]{3,2,1,0:T(8,128)S(1)} %shard_map.46) | data formatting | bytes 163840
Async XLA Ops:
  0.0 0.7 %copy-start.3 = (f32[9]{0:T(128)S(1)}, f32[9]{0:T(128)}, u32[]{:S(2)}) copy-start(f32[9]{0:T(128)} %spatial.1) | copy-start | bytes 112
  0.0 0.7 %copy-start.2 = (f32[60]{0:T(128)S(1)}, f32[60]{0:T(128)}, u32[]{:S(2)}) copy-start(f32[60]{0:T(128)} %param.5) | copy-start | bytes 724
  0.7 1.2 %copy-start = (bf16[16,32768]{1,0:T(8,128)(2,1)S(1)}, bf16[16,32768]{1,0:T(8,128)(2,1)}, u32[]{:S(2)}) copy-start(bf16[16,32768]{1,0:T(8,128)(2,1)} %strain.1) | copy-start | bytes 3145732
  1.9 1.1 %copy-start.1 = (bf16[320,1024]{1,0:T(8,128)(2,1)S(1)}, bf16[320,1024]{1,0:T(8,128)(2,1)}, u32[]{:S(2)}) copy-start(bf16[320,1024]{1,0:T(8,128)(2,1)} %constant.2.clone.table) | copy-start | bytes 1966084

commit v2 on v1

--- a/solution.py
+++ b/solution.py
@@ -53,8 +53,8 @@
 
 
 def kernel(
-    chans, reps, strain, taps, spatial, table, out,
-    own, rim, fir_w, fold_w, tab, filt, raw, power_low, own_raw, packs, gathered, tiles,
+    chans, reps, strain, taps_in, spatial_in, table, out,
+    taps, spatial, own, rim, fir_w, fold_w, tab, filt, raw, power_low, own_raw, packs, gathered, tiles,
     local_sem, rim_send, rim_recv, hist_send, hist_recv, one_send, one_recv, two_send, two_recv,
 ):
     b = lax.axis_index("chan")
@@ -78,10 +78,40 @@
         )
     fetch_own = pltpu.make_async_copy(strain, own.at[:, pl.ds(LANES, samples)], local_sem.at[0])
     fetch_own.start()
+    fetch_spatial = pltpu.make_async_copy(spatial_in, spatial, local_sem.at[2])
+    fetch_spatial.start()
+    fetch_taps = pltpu.make_async_copy(taps_in, taps, local_sem.at[3])
+    fetch_taps.start()
     fetch_tab = pltpu.make_async_copy(table, tab, local_sem.at[1])
     fetch_tab.start()
 
+    pl.semaphore_wait(barrier, len(peers))
+
+    def rim_copy(k):
+        return pltpu.make_async_remote_copy(
+            strain.at[pl.ds(0, 8), pl.ds(k * span, span)],
+            rim.at[:, pl.ds(pl.multiple_of(LANES + k * span, LANES), span)],
+            rim_send.at[k], rim_recv.at[k],
+            device_id={"chan": block_at(-1), "rep": r}, device_id_type=MESH,
+        )
+
+    hist_own = pltpu.make_async_remote_copy(
+        strain.at[:, pl.ds(samples - LANES, LANES)], own.at[:, pl.ds(0, LANES)],
+        hist_send.at[0], hist_recv.at[0],
+        device_id={"chan": b, "rep": rep_at(1)}, device_id_type=MESH,
+    )
+    hist_rim = pltpu.make_async_remote_copy(
+        strain.at[pl.ds(0, 8), pl.ds(samples - LANES, LANES)], rim.at[:, pl.ds(0, LANES)],
+        hist_send.at[1], hist_recv.at[1],
+        device_id={"chan": block_at(-1), "rep": rep_at(1)}, device_id_type=MESH,
+    )
+    hist_own.start()
+    hist_rim.start()
+    for k in range(chunks):
+        rim_copy(k).start()
+
     row, lane = iota((LANES, LANES), 0), iota((LANES, LANES), 1)
+    fetch_taps.wait()
     tap_row = jnp.concatenate([taps[...], jnp.zeros((1, LANES - taps.shape[1]), F32)], axis=1)
     circulant = pltpu.roll(jnp.broadcast_to(tap_row, (LANES, LANES)), 0, 1, stride=1, stride_axis=0)
     now = jnp.where(lane >= row, circulant, 0.0)
@@ -107,6 +137,7 @@
         fold_w[q * LANES : (q + 1) * LANES, LANES:] = (part - part_high.astype(F32)).astype(BF16)
 
     half_row = iota((8, LANES), 0)
+    fetch_spatial.wait()
     weights = [spatial[j] for j in range(9)]
     crossing = []
     for j in range(9):
@@ -114,36 +145,6 @@
         keep = jnp.logical_or(same, b != chans - 1)
         crossing.append(jnp.where(keep, weights[j], 0.0))
 
-    pl.semaphore_wait(barrier, len(peers))
-
-    rim_copies = []
-    for k in range(chunks):
-        if k == 0:
-            source = strain.at[pl.ds(0, 8), pl.ds(0, span)]
-            target = rim.at[k, :, pl.ds(LANES, span)]
-        else:
-            source = strain.at[pl.ds(0, 8), pl.ds(k * span - LANES, span + LANES)]
-            target = rim.at[k]
-        rim_copies.append(
-            pltpu.make_async_remote_copy(
-                source, target, rim_send.at[k], rim_recv.at[k],
-                device_id={"chan": block_at(-1), "rep": r}, device_id_type=MESH,
-            )
-        )
-    hist_own = pltpu.make_async_remote_copy(
-        strain.at[:, pl.ds(samples - LANES, LANES)], own.at[:, pl.ds(0, LANES)],
-        hist_send.at[0], hist_recv.at[0],
-        device_id={"chan": b, "rep": rep_at(1)}, device_id_type=MESH,
-    )
-    hist_rim = pltpu.make_async_remote_copy(
-        strain.at[pl.ds(0, 8), pl.ds(samples - LANES, LANES)], rim.at[0, :, pl.ds(0, LANES)],
-        hist_send.at[1], hist_recv.at[1],
-        device_id={"chan": block_at(-1), "rep": rep_at(1)}, device_id_type=MESH,
-    )
-    hist_own.start()
-    hist_rim.start()
-    for k in reversed(range(chunks)):
-        rim_copies[k].start()
     fetch_own.wait()
 
     def lower_window(w):
@@ -168,9 +169,9 @@
             lower_window(first + t)
             return carry
 
-        lax.fori_loop(0, CW, body, 0)
+        lax.fori_loop(0, CW, body, 0, unroll=2)
         left = jnp.concatenate(
-            [own[:, pl.ds((first + t) * NFFT, NFFT + LANES)] for t in range(CW)], axis=0
+            [own[:, pl.ds(pl.multiple_of((first + t) * NFFT, LANES), NFFT + LANES)] for t in range(CW)], axis=0
         )
         parts = dot(left, fold_w[...])
         own_raw[k] = parts[:, 0:LANES] + parts[:, LANES:]
@@ -180,9 +181,9 @@
 
         def body(t, carry):
             w = first + t
-            base = pl.multiple_of(t * NFFT, LANES)
+            base = pl.multiple_of(w * NFFT, LANES)
             left = jnp.concatenate(
-                [rim[k, :, pl.ds(base + i * LANES, 2 * LANES)] for i in range(BLOCKS_PER_WINDOW)], axis=0
+                [rim[:, pl.ds(base + i * LANES, 2 * LANES)] for i in range(BLOCKS_PER_WINDOW)], axis=0
             )
             both_parts = dot(left, fir_w[...])
             band = both_parts[:, 0:LANES] + both_parts[:, LANES:]
@@ -197,8 +198,8 @@
             raw[t, 24:32, :] = squares
             return carry
 
-        lax.fori_loop(0, CW, body, 0)
-        left = jnp.concatenate([rim[k, :, pl.ds(t * NFFT, NFFT + LANES)] for t in range(CW)], axis=0)
+        lax.fori_loop(0, CW, body, 0, unroll=2)
+        left = jnp.concatenate([rim[:, pl.ds(pl.multiple_of((first + t) * NFFT, LANES), NFFT + LANES)] for t in range(CW)], axis=0)
         parts = dot(left, fold_w[...])
         rim_raw = parts[:, 0:LANES] + parts[:, LANES:]
         pieces = []
@@ -244,9 +245,11 @@
             device_id={"chan": block_at(1 if s == 0 else -s), "rep": r}, device_id_type=MESH,
         )
 
-    order = list(reversed(range(chunks)))
-    for k in order:
-        if k == 0:
+    def lower_body(step, carry):
+        k = lax.rem(step + 1, chunks)
+
+        @pl.when(step == chunks - 1)
+        def _():
             hist_own.wait_recv()
 
             @pl.when(r == 0)
@@ -254,6 +257,9 @@
                 own[:, 0:LANES] = jnp.zeros((16, LANES), BF16)
 
         lower_chunk(k)
+        return carry
+
+    lax.fori_loop(0, chunks, lower_body, 0)
 
     def forward(k):
         for d in range(1, reps):
@@ -261,22 +267,27 @@
         for s in range(5):
             second_copy(k, s).start()
 
-    for place, k in enumerate(order):
-        rim_copies[k].wait_recv()
-        if k == 0:
-            hist_rim.wait_recv()
-
-            @pl.when(r == 0)
-            def _():
-                rim[0, :, 0:LANES] = jnp.zeros((8, LANES), BF16)
-
+    hist_rim.wait_recv()
+
+    @pl.when(r == 0)
+    def _():
+        rim[:, 0:LANES] = jnp.zeros((8, LANES), BF16)
+
+    def upper_body(k, carry):
+        rim_copy(k).wait_recv()
         upper_chunk(k)
         for d in range(1, reps):
             first_copy(k, d).start()
-        if place > 0:
-            forward(order[place - 1])
-    forward(order[-1])
-    for k in order:
+
+        @pl.when(k > 0)
+        def _():
+            forward(k - 1)
+
+        return carry
+
+    lax.fori_loop(0, chunks, upper_body, 0)
+    forward(chunks - 1)
+    for k in range(chunks):
         for s in range(5):
             second_copy(k, s).wait_recv()
 
@@ -315,7 +326,7 @@
             out[c, s] = tile[c * GROUP : (c + 1) * GROUP, 0:32]
 
     for k in range(chunks):
-        rim_copies[k].wait_send()
+        rim_copy(k).wait_send()
         for d in range(1, reps):
             first_copy(k, d).wait_send()
         for s in range(5):
@@ -331,17 +342,17 @@
         rows, samples = strain.shape
         windows = samples // NFFT
         chunks = windows // CW
-        span = CW * NFFT
         anywhere = pl.BlockSpec(memory_space=pl.ANY)
-        vmem = pl.BlockSpec(memory_space=pltpu.VMEM)
         return pl.pallas_call(
             functools.partial(kernel, chans, reps),
             out_shape=jax.ShapeDtypeStruct((rows, 5, BINS // reps, 32), F32),
-            in_specs=[anywhere, vmem, pl.BlockSpec(memory_space=pltpu.SMEM), anywhere],
-            out_specs=vmem,
+            in_specs=[anywhere] * 4,
+            out_specs=pl.BlockSpec(memory_space=pltpu.VMEM),
             scratch_shapes=[
+                pltpu.VMEM((1, fir_taps.shape[0]), F32),
+                pltpu.SMEM(spatial.shape, F32),
                 pltpu.VMEM((rows, samples + LANES), BF16),
-                pltpu.VMEM((chunks, 8, span + LANES), BF16),
+                pltpu.VMEM((8, samples + LANES), BF16),
                 pltpu.VMEM((2 * LANES, 2 * LANES), BF16),
                 pltpu.VMEM((NFFT + LANES, 2 * LANES), BF16),
                 pltpu.VMEM((2 * LANES + 2 * BINS, 1024), BF16),
@@ -352,7 +363,7 @@
                 pltpu.VMEM((chunks, reps, 16, LANES), BF16),
                 pltpu.VMEM((6, chunks, reps, 16, LANES), BF16),
                 pltpu.VMEM((8, LANES), F32),
-                pltpu.SemaphoreType.DMA((2,)),
+                pltpu.SemaphoreType.DMA((4,)),
                 pltpu.SemaphoreType.DMA((chunks,)),
                 pltpu.SemaphoreType.DMA((chunks,)),
                 pltpu.SemaphoreType.DMA((2,)),
@@ -363,7 +374,7 @@
                 pltpu.SemaphoreType.DMA((chunks, 5)),
             ],
             compiler_params=pltpu.CompilerParams(
-                collective_id=0, has_side_effects=True, vmem_limit_bytes=40 * 1024 * 1024
+                collective_id=0, has_side_effects=True, vmem_limit_bytes=67043328
             ),
         )(strain, fir_taps.reshape(1, -1), spatial, jnp.asarray(tables()))
 

time: 52.4 us -> 49.4 us (0.943)
  local copies, waits for them, and re-layouts: 3.71 us -> 1.72 us
  Pallas kernels: 48.5 us -> 47.5 us
    unnamed x9 -> x1, local copies, waits for them, and re-layouts: 3.71 us -> 1.72 us
    pallas_call x1, Pallas kernels: 48.5 us -> 47.5 us  [per_device(): pl.pallas_call(functools.partial(kernel, chans, reps), out_shape=jax.Shap...]
where the time goes in v2:
time: 49.4 us; the launch traced here: 49.3 us
  Pallas kernels  47.5 us (96%)
  local copies, waits for them, and re-layouts  1.72 us (3%)
    pallas_call x1, Pallas kernels, per_device(): pl.pallas_call(functools.partial(kernel, chans, reps), out_shape=jax.Shap...  47.5 us
    unnamed x1, local copies, waits for them, and re-layouts  1.72 us

profile of v2, /device:TPU:1, one launch (start us, length us, event | category | flops | bytes accessed | tf_op | source)
XLA Modules:
  0.0 49.3 jit_solution(1301140221802382722)
XLA Ops:
  0.0 47.5 %shard_map.46 = f32[16,5,8,32]{3,2,1,0:T(8,128)} custom-call(bf16[16,32768]{1,0:T(8,128)(2,1)} %strain.1, f32[1,60]{1,0:T(1,128)} %bitcast.1, f32[9]{0:T(128)} %spatial_in.1, bf16[320,1024]{1,0:T(8,128)(2,1)} %constant.2.clone.table), custom_call_target="tpu_custom_call" | custom-call | tf_op jit(solution)/shard_map/pallas_call | solution.py:346
  47.5 1.7 %copy.6 = f32[16,5,8,32]{3,2,1,0:T(8,128)} copy(f32[16,5,8,32]{3,2,1,0:T(8,128)} %shard_map.46) | data formatting | bytes 163840

commit v3 on v2

--- a/solution.py
+++ b/solution.py
@@ -54,7 +54,7 @@
 
 def kernel(
     chans, reps, strain, taps_in, spatial_in, table, out,
-    taps, spatial, own, rim, fir_w, fold_w, tab, filt, raw, power_low, own_raw, packs, gathered, tiles,
+    taps, spatial, own, rim, fir_w, fold_w, tab, filt, raw, power_low, own_raw, packs, gathered, near, near_in,
     local_sem, rim_send, rim_recv, hist_send, hist_recv, one_send, one_recv, two_send, two_recv,
 ):
     b = lax.axis_index("chan")
@@ -230,19 +230,19 @@
         packed = dot(collect, stacked).astype(BF16)
         for g in range(reps):
             packs[k, g] = packed[:, g * LANES : (g + 1) * LANES]
-        gathered[1, k, r] = packs[k, r]
+        gathered[0, k, r] = packs[k, r]
 
     def first_copy(k, d):
         return pltpu.make_async_remote_copy(
-            packs.at[k, rep_at(d)], gathered.at[1, k, r], one_send.at[k, d - 1], one_recv.at[k, d - 1],
+            packs.at[k, rep_at(d)], gathered.at[0, k, r], one_send.at[k, d - 1], one_recv.at[k, d - 1],
             device_id={"chan": b, "rep": rep_at(d)}, device_id_type=MESH,
         )
 
     def second_copy(k, s):
-        slot = 0 if s == 0 else s + 1
+        source, target, step = (near, near_in, 1) if s == 0 else (gathered.at[0], gathered.at[s], -s)
         return pltpu.make_async_remote_copy(
-            gathered.at[1, k], gathered.at[slot, k], two_send.at[k, s], two_recv.at[k, s],
-            device_id={"chan": block_at(1 if s == 0 else -s), "rep": r}, device_id_type=MESH,
+            source.at[k], target.at[k], two_send.at[k, s], two_recv.at[k, s],
+            device_id={"chan": block_at(step), "rep": r}, device_id_type=MESH,
         )
 
     def lower_body(step, carry):
@@ -264,8 +264,15 @@
     def forward(k):
         for d in range(1, reps):
             first_copy(k, d).wait_recv()
-        for s in range(5):
+        for s in range(1, 5):
             second_copy(k, s).start()
+        quarter = iota((16, LANES), 1) // 32
+        side = jnp.zeros((16, LANES), F32)
+        for g in range(reps):
+            part = gathered[0, k, g].astype(F32)
+            side = jnp.where(quarter == g, part if g == 0 else pltpu.roll(part, 32 * g, 1), side)
+        near[k] = side.astype(BF16)
+        second_copy(k, 0).start()
 
     hist_rim.wait_recv()
 
@@ -278,15 +285,11 @@
         upper_chunk(k)
         for d in range(1, reps):
             first_copy(k, d).start()
-
-        @pl.when(k > 0)
-        def _():
-            forward(k - 1)
-
         return carry
 
     lax.fori_loop(0, chunks, upper_body, 0)
-    forward(chunks - 1)
+    for k in range(chunks):
+        forward(k)
     for k in range(chunks):
         for s in range(5):
             second_copy(k, s).wait_recv()
@@ -294,14 +297,18 @@
     depth = chunks * reps * 16
     own_lanes = iota((depth, LANES), 1) < 32
 
+    def block_of(s):
+        return gathered[s].reshape(depth, LANES).astype(F32)
+
     def merged(s):
-        return jnp.where(
-            own_lanes,
-            gathered[s].reshape(depth, LANES).astype(F32),
-            gathered[s + 1].reshape(depth, LANES).astype(F32),
-        )
-
-    mine = merged(0)
+        return jnp.where(own_lanes, block_of(s - 1), block_of(s))
+
+    own_first = []
+    for k in range(chunks):
+        side = near_in[k].astype(F32)
+        for g in range(reps):
+            own_first.append(side if g == 0 else pltpu.roll(side, LANES - 32 * g, 1))
+    mine = jnp.where(own_lanes, jnp.concatenate(own_first, axis=0), block_of(0))
     cubes = mine.reshape(chunks * reps, 2, 8, LANES)
     swapped = jnp.concatenate([cubes[:, 1:2], -cubes[:, 0:1]], axis=1).reshape(depth, LANES)
     left = jnp.concatenate([mine.T, swapped.T], axis=0).astype(BF16)
@@ -361,8 +368,9 @@
                 pltpu.VMEM((windows, 8, LANES), F32),
                 pltpu.VMEM((chunks, CW * 16, LANES), F32),
                 pltpu.VMEM((chunks, reps, 16, LANES), BF16),
-                pltpu.VMEM((6, chunks, reps, 16, LANES), BF16),
-                pltpu.VMEM((8, LANES), F32),
+                pltpu.VMEM((5, chunks, reps, 16, LANES), BF16),
+                pltpu.VMEM((chunks, 16, LANES), BF16),
+                pltpu.VMEM((chunks, 16, LANES), BF16),
                 pltpu.SemaphoreType.DMA((4,)),
                 pltpu.SemaphoreType.DMA((chunks,)),
                 pltpu.SemaphoreType.DMA((chunks,)),

time: 49.4 us -> 49.1 us (level)
  no operation moved by 1% of the time
where the time goes in v3:
time: 49.1 us; the launch traced here: 49 us
  Pallas kernels  47.2 us (96%)
  local copies, waits for them, and re-layouts  1.72 us (4%)
    pallas_call x1, Pallas kernels, per_device(): pl.pallas_call(functools.partial(kernel, chans, reps), out_shape=jax.Shap...  47.2 us
    unnamed x1, local copies, waits for them, and re-layouts  1.72 us

profile of v3, /device:TPU:1, one launch (start us, length us, event | category | flops | bytes accessed | tf_op | source)
XLA Modules:
  0.0 49.0 jit_solution(6107241921429354939)
XLA Ops:
  0.0 47.2 %shard_map.46 = f32[16,5,8,32]{3,2,1,0:T(8,128)} custom-call(bf16[16,32768]{1,0:T(8,128)(2,1)} %strain.1, f32[1,60]{1,0:T(1,128)} %bitcast.1, f32[9]{0:T(128)} %spatial_in.1, bf16[320,1024]{1,0:T(8,128)(2,1)} %constant.2.clone.table), custom_call_target="tpu_custom_call" | custom-call | tf_op jit(solution)/shard_map/pallas_call | solution.py:353
  47.2 1.7 %copy.6 = f32[16,5,8,32]{3,2,1,0:T(8,128)} copy(f32[16,5,8,32]{3,2,1,0:T(8,128)} %shard_map.46) | data formatting | bytes 163840

commit v4 on v2

--- a/solution.py
+++ b/solution.py
@@ -169,7 +169,7 @@
             lower_window(first + t)
             return carry
 
-        lax.fori_loop(0, CW, body, 0, unroll=2)
+        lax.fori_loop(0, CW, body, 0, unroll=4)
         left = jnp.concatenate(
             [own[:, pl.ds(pl.multiple_of((first + t) * NFFT, LANES), NFFT + LANES)] for t in range(CW)], axis=0
         )
@@ -198,7 +198,7 @@
             raw[t, 24:32, :] = squares
             return carry
 
-        lax.fori_loop(0, CW, body, 0, unroll=2)
+        lax.fori_loop(0, CW, body, 0, unroll=4)
         left = jnp.concatenate([rim[:, pl.ds(pl.multiple_of((first + t) * NFFT, LANES), NFFT + LANES)] for t in range(CW)], axis=0)
         parts = dot(left, fold_w[...])
         rim_raw = parts[:, 0:LANES] + parts[:, LANES:]
@@ -278,15 +278,11 @@
         upper_chunk(k)
         for d in range(1, reps):
             first_copy(k, d).start()
-
-        @pl.when(k > 0)
-        def _():
-            forward(k - 1)
-
         return carry
 
     lax.fori_loop(0, chunks, upper_body, 0)
-    forward(chunks - 1)
+    for k in range(chunks):
+        forward(k)
     for k in range(chunks):
         for s in range(5):
             second_copy(k, s).wait_recv()

time: 49.4 us -> 48.3 us (0.978)
  Pallas kernels: 47.5 us -> 46.5 us
    pallas_call x1, Pallas kernels: 47.5 us -> 46.5 us  [per_device(): pl.pallas_call(functools.partial(kernel, chans, reps), out_shape=jax.Shap...]
where the time goes in v4:
time: 48.3 us; the launch traced here: 48.2 us
  Pallas kernels  46.5 us (96%)
  local copies, waits for them, and re-layouts  1.72 us (4%)
    pallas_call x1, Pallas kernels, per_device(): pl.pallas_call(functools.partial(kernel, chans, reps), out_shape=jax.Shap...  46.5 us
    unnamed x1, local copies, waits for them, and re-layouts  1.72 us

profile of v4, /device:TPU:1, one launch (start us, length us, event | category | flops | bytes accessed | tf_op | source)
XLA Modules:
  0.0 48.2 jit_solution(9246137362153664605)
XLA Ops:
  0.0 46.5 %shard_map.46 = f32[16,5,8,32]{3,2,1,0:T(8,128)} custom-call(bf16[16,32768]{1,0:T(8,128)(2,1)} %strain.1, f32[1,60]{1,0:T(1,128)} %bitcast.1, f32[9]{0:T(128)} %spatial_in.1, bf16[320,1024]{1,0:T(8,128)(2,1)} %constant.2.clone.table), custom_call_target="tpu_custom_call" | custom-call | tf_op jit(solution)/shard_map/pallas_call | solution.py:342
  46.5 1.7 %copy.6 = f32[16,5,8,32]{3,2,1,0:T(8,128)} copy(f32[16,5,8,32]{3,2,1,0:T(8,128)} %shard_map.46) | data formatting | bytes 163840
